TPU v7x, 512 devices: a whole 4x8x8 slice. The times are simulated.
512 devices in a mesh: section: 8 (over y), dp: 64 (over z, x, core).
Axes of the slice: x: 4, y: 8, z: 8, core: 2. Of those that a mesh axis runs over, the one named last changes fastest.
Arguments:
- fresh_acts: bfloat16 [3, 128, 8192], P(None, None, 'dp'), may hold values from -36 to 36
- carried: bfloat16 [8, 128, 8192], P('section', None, 'dp'), may hold values from -36 to 36
- norm_gain: float32 [8, 8192], P('section'), may hold values from 0.1 to 1.9
- w_in: bfloat16 [8, 3, 4096, 8192], P('section', None, 'dp'), may hold values from -0.0625 to 0.0625
- short_filter: float32 [8, 3, 4096, 3], P('section', None, 'dp'), may hold values from -3 to 3
- filter_taps: float32 [8, 4096, 128], P('section', 'dp'), may hold values from -0.9 to 0.9
- decay_rate: float32 [8, 4096], P('section', 'dp'), may hold values from 0.01 to 0.12
- w_out: bfloat16 [8, 4096, 8192], P('section', None, 'dp'), may hold values from -0.09375 to 0.09375
Outputs:
- section_outputs: bfloat16 [8, 3, 128, 8192], P('section', None, None, 'dp')
All inputs are finite; a program needn't handle non-finite values.
Results may differ from a plain program's by a relative error of at most 0.011.
Values may be sent and summed in bfloat16 or wider, within the bound.
A program may use at most 64 MiB of HBM per device.

v0:
```python
import jax
import jax.numpy as jnp
from jax import lax
from jax.sharding import PartitionSpec as P

EPS = 1e-06


def shifted(value, axis, steps):
    count = lax.axis_size(axis)
    pairs = [(source, (source + steps) % count) for source in range(count)]
    return lax.ppermute(value, axis, pairs)


def build_toeplitz(tap_values, decay_rate, tok_len):
    tap_count = tap_values.shape[1]
    lag_grid = jnp.arange(tok_len)[:, None] - jnp.arange(tok_len)[None, :]
    onehot = (lag_grid[:, :, None] == jnp.arange(tap_count)[None, None, :]).astype(jnp.float32)
    filter_vals = tap_values * jnp.exp(
        -decay_rate[:, None] * jnp.arange(tap_count, dtype=jnp.float32)[None, :]
    )
    return jnp.einsum("cj,tsj->cts", filter_vals, onehot, precision=lax.Precision.HIGHEST)


def mixing(u_proj, short_taps, toeplitz):
    tok_len = u_proj.shape[0]
    tap_count = short_taps.shape[2]
    padded = jnp.pad(u_proj, ((tap_count - 1, 0), (0, 0), (0, 0)))
    mixed_out = short_taps[:, :, 0] * u_proj
    for j in range(1, tap_count):
        mixed_out = (
            mixed_out
            + short_taps[:, :, j] * padded[tap_count - 1 - j : tap_count - 1 - j + tok_len]
        )
    query_part = mixed_out[:, 0]
    product = mixed_out[:, 1] * mixed_out[:, 2]
    long_conv = jnp.einsum("cts,sc->tc", toeplitz, product, precision=lax.Precision.HIGHEST)
    return (query_part * long_conv).astype(jnp.bfloat16)


def contract_rows(normed, weight_rows):
    return lax.dot_general(
        normed, weight_rows, (((1,), (1,)), ((), ())), preferred_element_type=jnp.float32
    )


def body(fresh_acts, carried, norm_gain, w_in, short_filter, filter_taps, decay_rate, w_out):
    section_idx = lax.axis_index("section")
    section_count = lax.axis_size("section")
    is_first = section_idx == 0
    tick_count = fresh_acts.shape[0]
    tok_len = fresh_acts.shape[1]
    feat_dev = fresh_acts.shape[2]
    model_width = norm_gain.shape[1]
    chan_dev = w_in.shape[2]
    gain_row = norm_gain[0]
    w_in_flat = w_in[0].reshape(3 * chan_dev, model_width)
    w_out_local = w_out[0]
    short_taps = short_filter[0]
    toeplitz = build_toeplitz(filter_taps[0], decay_rate[0], tok_len)
    own_start = lax.axis_index("dp") * feat_dev
    start_slice = jnp.where(is_first, fresh_acts[0], carried[0])
    results = []
    is_last = section_idx == section_count - 1
    full_rows = lax.all_gather(start_slice, "dp", axis=1, tiled=True)
    for k in range(tick_count):
        widened = full_rows.astype(jnp.float32)
        normed = (widened * gain_row).astype(jnp.bfloat16)
        from_proj_acc = contract_rows(normed, w_in_flat)
        from_sum_sq = jnp.sum(widened * widened, axis=1)
        from_own_slice = lax.dynamic_slice_in_dim(full_rows, own_start, feat_dev, 1)
        factor = lax.rsqrt(from_sum_sq / model_width + EPS)
        u_proj = (from_proj_acc * factor[:, None]).reshape(tok_len, 3, chan_dev)
        y_local = mixing(u_proj, short_taps, toeplitz)
        out_acc = jnp.dot(
            lax.all_gather(y_local, "dp", axis=1, tiled=True),
            w_out_local,
            preferred_element_type=jnp.float32,
        )
        produced = (from_own_slice.astype(jnp.float32) + out_acc).astype(jnp.bfloat16)
        results.append(produced)
        if k + 1 < tick_count:
            source = jnp.where(is_last, fresh_acts[k + 1], produced)
            gathered = lax.all_gather(source, "dp", axis=1, tiled=True)
            full_rows = shifted(gathered, "section", 1)
    return jnp.stack(results)[None]


def solution(mesh):
    return jax.shard_map(
        body,
        mesh=mesh,
        in_specs=(
            P(None, None, "dp"),
            P("section", None, "dp"),
            P("section", None),
            P("section", None, "dp", None),
            P("section", None, "dp", None),
            P("section", "dp", None),
            P("section", "dp"),
            P("section", None, "dp"),
        ),
        out_specs=P("section", None, None, "dp"),
        check_vma=False,
    )
```

profile of v0, /device:TPU:1, one launch (start us, length us, event | category | flops | bytes accessed | tf_op | source)
XLA Modules:
  0.0 632.6 jit_solution(17019697142126312985)
XLA Ops:
  6.5 1.5 slice_select_fusion
  8.1 0.0 all-gather.18.cloned.1.call-update
  8.1 0.0 all-gather.8.cloned.1.call-start
  8.1 0.7 copy.24
  8.9 0.7 negate_bitcast_fusion
  9.5 8.1 %fusion = f32[64,128,128]{2,0,1:T(8,128)} fusion(s32[128,128]{1,0:T(8,128)S(1)} %iota_subtract_fusion, f32[1,64,128]{2,1,0:T(8,128)} %param.13, f32[64]{0:T(128)S(1)} %negate_bitcast_fusion), kind=kOutput, calls=%fused_computation.1 | convolution fusion | flops 1612726272 | bytes 4292864 | tf_op jit(solution)/shard_map/cj,tsj->cts/dot_general | solution.py:22
  17.6 5.4 copy.10
  23.0 72.1 %all-gather.18.cloned.1.call-done = bf16[1,128,8192]{2,1,0:T(8,128)(2,1)} async-done(((bf16[1,128,128]{2,1,0:T(8,128)(2,1)}), bf16[1,128,8192]{2,1,0:T(8,128)(2,1)}) %all-gather.18.cloned.1.call-update) | async-done | bytes 2097168 | tf_op jit(solution)/shard_map/all_gather | solution.py:65
  95.1 2.1 fusion.6
  97.2 2.7 fusion.24
  100.0 0.0 copy-start.6
  100.0 0.2 fusion.35
  100.2 3.7 fusion.60
  103.9 0.6 fusion.51
  104.5 0.0 all-gather.8.cloned.1.call-update
  104.5 0.0 all-gather.10.cloned.1.call-start
  104.6 81.2 %all-gather.8.cloned.1.call-done = bf16[128,4096]{0,1:T(8,128)(2,1)} async-done(((bf16[128,64]{0,1:T(8,128)(2,1)}), bf16[128,4096]{0,1:T(8,128)(2,1)}) %all-gather.8.cloned.1.call-update) | async-done | bytes 1048592 | tf_op jit(solution)/shard_map/all_gather | solution.py:76
  185.8 2.6 bitcast_select_fusion.1
  188.5 0.0 all-gather.10.cloned.1.call-update
  188.5 0.0 all-gather.12.cloned.1.call-start
  188.5 76.4 %all-gather.10.cloned.1.call-done = bf16[128,8192]{1,0:T(8,128)(2,1)} async-done(((bf16[128,128]{1,0:T(8,128)(2,1)}), bf16[128,8192]{1,0:T(8,128)(2,1)}) %all-gather.10.cloned.1.call-update) | async-done | bytes 2097168 | tf_op jit(solution)/shard_map/all_gather | solution.py:84
  264.9 3.3 collective-permute-start
  268.2 47.0 %collective-permute-done = bf16[128,8192]{1,0:T(8,128)(2,1)S(1)} collective-permute-done((bf16[128,8192]{1,0:T(8,128)(2,1)}, bf16[128,8192]{1,0:T(8,128)(2,1)S(1)}, u32[]{:S(2)}, u32[]{:S(2)}) %collective-permute-start) | collective-permute-done | bytes 2097184 | tf_op jit(solution)/shard_map/ppermute | solution.py:12
  315.2 0.5 fusion.2
  315.7 1.1 fusion.18
  316.8 0.2 fusion.39
  317.0 1.1 copy-done.2
  318.1 3.6 fusion.61
  321.8 0.6 fusion.49
  322.4 0.0 all-gather.12.cloned.1.call-update
  322.4 0.0 all-gather.14.cloned.1.call-start
  322.5 82.1 %all-gather.12.cloned.1.call-done = bf16[128,4096]{0,1:T(8,128)(2,1)} async-done(((bf16[128,64]{0,1:T(8,128)(2,1)}), bf16[128,4096]{0,1:T(8,128)(2,1)}) %all-gather.12.cloned.1.call-update) | async-done | bytes 1048592 | tf_op jit(solution)/shard_map/all_gather | solution.py:76
  404.5 2.6 bitcast_select_fusion
  407.2 0.0 all-gather.14.cloned.1.call-update
  407.2 0.0 all-gather.16.cloned.1.call-start
  407.3 76.3 %all-gather.14.cloned.1.call-done = bf16[128,8192]{1,0:T(8,128)(2,1)} async-done(((bf16[128,128]{1,0:T(8,128)(2,1)}), bf16[128,8192]{1,0:T(8,128)(2,1)}) %all-gather.14.cloned.1.call-update) | async-done | bytes 2097168 | tf_op jit(solution)/shard_map/all_gather | solution.py:84
  483.5 3.1 collective-permute-start.1
  486.6 47.2 %collective-permute-done.1 = bf16[128,8192]{1,0:T(8,128)(2,1)S(1)} collective-permute-done((bf16[128,8192]{1,0:T(8,128)(2,1)}, bf16[128,8192]{1,0:T(8,128)(2,1)S(1)}, u32[]{:S(2)}, u32[]{:S(2)}) %collective-permute-start.1) | collective-permute-done | bytes 2097184 | tf_op jit(solution)/shard_map/ppermute | solution.py:12
  533.8 0.5 fusion.4
  534.3 1.1 fusion.21
  535.4 0.2 fusion.43
  535.6 1.1 copy-done.3
  536.7 3.6 fusion.62
  540.4 0.6 fusion.47
  541.0 0.0 all-gather.16.cloned.1.call-update
  541.0 82.1 %all-gather.16.cloned.1.call-done = bf16[128,4096]{0,1:T(8,128)(2,1)} async-done(((bf16[128,64]{0,1:T(8,128)(2,1)}), bf16[128,4096]{0,1:T(8,128)(2,1)}) %all-gather.16.cloned.1.call-update) | async-done | bytes 1048592 | tf_op jit(solution)/shard_map/all_gather | solution.py:76
  623.1 2.0 fusion.45
  625.1 0.7 maximum_bitcast_fusion
  (24 shorter events, 0.1 us)
Async XLA Ops:
  6.5 90.7 %copy-start = (bf16[1,3,64,8192]{3,2,1,0:T(8,128)(2,1)S(1)}, bf16[1,3,64,8192]{3,2,1,0:T(8,128)(2,1)}, u32[]{:S(2)}) copy-start(bf16[1,3,64,8192]{3,2,1,0:T(8,128)(2,1)} %param.11) | copy-start | bytes 9437188
  6.5 88.6 %all-gather.18.cloned.1.call-start = ((), (), s32[]{:S(2)}) async-start(), calls=%async_computation.5 | async-start | bytes 2129920 | tf_op jit(solution)/shard_map/all_gather | solution.py:65
  8.1 177.7 %all-gather.8.cloned.1.call-start = ((), (), s32[]{:S(2)}) async-start(), calls=%async_computation | async-start | bytes 1064960 | tf_op jit(solution)/shard_map/all_gather | solution.py:76
  17.6 79.6 %copy-start.7 = (f32[1,8192]{1,0:T(1,128)S(1)}, f32[1,8192]{1,0:T(1,128)}, u32[]{:S(2)}) copy-start(f32[1,8192]{1,0:T(1,128)} %param.10) | copy-start | bytes 98308
  97.2 3.0 copy-start.1
  100.0 85.8 %copy-start.6 = (bf16[3,128,128]{2,1,0:T(8,128)(2,1)S(1)}, bf16[3,128,128]{2,1,0:T(8,128)(2,1)}, u32[]{:S(2)}) copy-start(bf16[3,128,128]{2,1,0:T(8,128)(2,1)} %param.8) | copy-start | bytes 294916
  104.5 160.4 %all-gather.10.cloned.1.call-start = ((), (), s32[]{:S(2)}) async-start(), calls=%async_computation.1 | async-start | bytes 2129920 | tf_op jit(solution)/shard_map/all_gather | solution.py:84
  188.5 216.1 %all-gather.12.cloned.1.call-start = ((), (), s32[]{:S(2)}) async-start(), calls=%async_computation.2 | async-start | bytes 1064960 | tf_op jit(solution)/shard_map/all_gather | solution.py:76
  264.9 50.3 %collective-permute-start = (bf16[128,8192]{1,0:T(8,128)(2,1)}, bf16[128,8192]{1,0:T(8,128)(2,1)S(1)}, u32[]{:S(2)}, u32[]{:S(2)}) collective-permute-start(bf16[128,8192]{1,0:T(8,128)(2,1)} %all-gather.10.cloned.1.call-done), channel_id=1, source_target_pairs={{0,64},{64,128},{128,192},{192,256},{256,320},{320,384},{384,448},... | collective-permute-start | bytes 6291464 | tf_op jit(solution)/shard_map/ppermute | solution.py:12
  315.2 1.6 copy-start.4
  315.7 2.4 copy-start.2
  322.4 161.1 %all-gather.14.cloned.1.call-start = ((), (), s32[]{:S(2)}) async-start(), calls=%async_computation.3 | async-start | bytes 2129920 | tf_op jit(solution)/shard_map/all_gather | solution.py:84
  407.2 215.9 %all-gather.16.cloned.1.call-start = ((), (), s32[]{:S(2)}) async-start(), calls=%async_computation.4 | async-start | bytes 1064960 | tf_op jit(solution)/shard_map/all_gather | solution.py:76
  483.5 50.3 %collective-permute-start.1 = (bf16[128,8192]{1,0:T(8,128)(2,1)}, bf16[128,8192]{1,0:T(8,128)(2,1)S(1)}, u32[]{:S(2)}, u32[]{:S(2)}) collective-permute-start(bf16[128,8192]{1,0:T(8,128)(2,1)} %all-gather.14.cloned.1.call-done), channel_id=1, source_target_pairs={{0,64},{64,128},{128,192},{192,256},{256,320},{320,384},{384,448},... | collective-permute-start | bytes 6291464 | tf_op jit(solution)/shard_map/ppermute | solution.py:12
  533.8 1.6 copy-start.5
  534.3 2.4 copy-start.3
Sparse Core Ops, SparseCore 0:
  10.6 84.5 all-gather.17
  104.6 81.1 all-gather.7
  189.0 75.8 all-gather.9
  322.6 81.9 all-gather.11
  407.6 75.8 all-gather.13
  541.1 81.9 all-gather.15
where the time goes:
time: 633 us
  waiting for transfers between devices  564 us (89%)
  matrix products  31.2 us (5%)
  between operations  13.7 us (2%)
  other arithmetic  8.37 us (1%)
  local copies, waits for them, and re-layouts  8.34 us (1%)
  starting transfers between devices  6.59 us (1%)
    all_gather x3, waiting for transfers between devices, body(): lax.all_gather(y_local, 'dp', axis=1, tiled=True)  245 us
    all_gather x2, waiting for transfers between devices, body(): gathered = lax.all_gather(source, 'dp', axis=1, tiled=True)  153 us
    ppermute x2, waiting for transfers between devices, shifted(): return lax.ppermute(value, axis, pairs)  94.2 us
    all_gather x1, waiting for transfers between devices, body(): full_rows = lax.all_gather(start_slice, 'dp', axis=1, tiled=True)  72.1 us
  transfers between devices with their start and end apart: 8, of which 8 were waited for; matrix products, arithmetic and copies ran while one was open for 2% of the time, Pallas kernels for 0%

commit v1 on v0

--- a/solution.py
+++ b/solution.py
@@ -81,7 +81,9 @@
         results.append(produced)
         if k + 1 < tick_count:
             source = jnp.where(is_last, fresh_acts[k + 1], produced)
-            gathered = lax.all_gather(source, "dp", axis=1, tiled=True)
+            gathered = jnp.concatenate(
+                lax.all_to_all(jnp.stack([source] * lax.axis_size("dp")), "dp", 0, 0), axis=1
+            )
             full_rows = shifted(gathered, "section", 1)
     return jnp.stack(results)[None]
 

time: 633 us -> 589 us (0.930)
  waiting for transfers between devices: 564 us -> 408 us
  blocking collectives: 0 us -> 112 us
    all_gather x2 -> x0, waiting for transfers between devices: 153 us -> none  [body(): gathered = lax.all_gather(source, 'dp', axis=1, tiled=True)]
    all_to_all x0 -> x2, blocking collectives: none -> 112 us  [body(): lax.all_to_all(jnp.stack([source] * lax.axis_size('dp')), 'dp', 0, 0)]
  transfers between devices with their start and end apart: 8 -> 6, of which waited for: 8 -> 6; matrix products, arithmetic and copies ran while one was open for 2% -> 3% of each run, Pallas kernels for 0% -> 0%
where the time goes in v1:
time: 589 us
  waiting for transfers between devices  408 us (69%)
  blocking collectives  112 us (19%)
  matrix products  30 us (5%)
  between operations  13.4 us (2%)
  local copies, waits for them, and re-layouts  9.97 us (2%)
  other arithmetic  8.37 us (1%)
  starting transfers between devices  6.76 us (1%)
    all_gather x3, waiting for transfers between devices, body(): lax.all_gather(y_local, 'dp', axis=1, tiled=True)  247 us
    all_to_all x2, blocking collectives, body(): lax.all_to_all(jnp.stack([source] * lax.axis_size('dp')), 'dp', 0, 0)  112 us
    ppermute x2, waiting for transfers between devices, shifted(): return lax.ppermute(value, axis, pairs)  89.5 us
    all_gather x1, waiting for transfers between devices, body(): full_rows = lax.all_gather(start_slice, 'dp', axis=1, tiled=True)  72.1 us
  transfers between devices with their start and end apart: 6, of which 6 were waited for; matrix products, arithmetic and copies ran while one was open for 3% of the time, Pallas kernels for 0%

profile of v1, /device:TPU:1, one launch (start us, length us, event | category | flops | bytes accessed | tf_op | source)
XLA Modules:
  0.0 588.8 jit_solution(3853755436859652920)
XLA Ops:
  6.5 1.5 slice_select_fusion
  8.1 0.0 all-gather.12.cloned.1.call-update
  8.1 0.0 all-gather.6.cloned.1.call-start
  8.1 0.7 copy.30
  8.9 0.7 negate_bitcast_fusion
  9.5 8.1 %fusion = f32[64,128,128]{2,0,1:T(8,128)} fusion(s32[128,128]{1,0:T(8,128)S(1)} %iota_subtract_fusion, f32[1,64,128]{2,1,0:T(8,128)} %param.13, f32[64]{0:T(128)S(1)} %negate_bitcast_fusion), kind=kOutput, calls=%fused_computation.1 | convolution fusion | flops 1612726272 | bytes 4292864 | tf_op jit(solution)/shard_map/cj,tsj->cts/dot_general | solution.py:22
  17.6 5.5 copy.12
  23.1 72.1 %all-gather.12.cloned.1.call-done = bf16[1,128,8192]{2,1,0:T(8,128)(2,1)} async-done(((bf16[1,128,128]{2,1,0:T(8,128)(2,1)}), bf16[1,128,8192]{2,1,0:T(8,128)(2,1)}) %all-gather.12.cloned.1.call-update) | async-done | bytes 2097168 | tf_op jit(solution)/shard_map/all_gather | solution.py:65
  95.1 2.1 fusion.6
  97.2 2.7 fusion.24
  100.0 0.0 copy-start.6
  100.0 0.2 fusion.35
  100.2 3.7 fusion.60
  103.9 0.6 fusion.51
  104.5 0.0 all-gather.6.cloned.1.call-update
  104.5 0.0 all-gather.8.cloned.1.call-start
  104.6 81.2 %all-gather.6.cloned.1.call-done = bf16[128,4096]{0,1:T(8,128)(2,1)} async-done(((bf16[128,64]{0,1:T(8,128)(2,1)}), bf16[128,4096]{0,1:T(8,128)(2,1)}) %all-gather.6.cloned.1.call-update) | async-done | bytes 1048592 | tf_op jit(solution)/shard_map/all_gather | solution.py:76
  185.8 2.0 bitcast_select_fusion.1
  187.8 0.5 stack.13
  188.3 56.0 %all_to_all.10 = bf16[64,128,128]{2,1,0:T(8,128)(2,1)S(1)} all-to-all(bf16[64,128,128]{2,1,0:T(8,128)(2,1)S(1)} %stack.13), channel_id=1, replica_groups=mesh['section'=8,'dp'=64] {'dp'}, dimensions={0} | all-to-all | bytes 4194304 | tf_op jit(solution)/shard_map/all_to_all | solution.py:85
  244.4 0.3 copy_bitcast_fusion.1
  244.7 3.3 collective-permute-start
  248.0 44.8 %collective-permute-done = bf16[128,8192]{1,0:T(8,128)(2,1)S(1)} collective-permute-done((bf16[128,8192]{1,0:T(8,128)(2,1)S(1)}, bf16[128,8192]{1,0:T(8,128)(2,1)S(1)}, u32[]{:S(2)}, u32[]{:S(2)}) %collective-permute-start) | collective-permute-done | bytes 2097184 | tf_op jit(solution)/shard_map/ppermute | solution.py:12
  292.8 0.5 fusion.2
  293.3 1.1 fusion.18
  294.4 0.2 fusion.39
  294.6 1.1 copy-done.2
  295.7 3.6 fusion.61
  299.3 0.6 fusion.49
  300.0 0.0 all-gather.8.cloned.1.call-update
  300.0 0.0 all-gather.10.cloned.1.call-start
  300.0 82.7 %all-gather.8.cloned.1.call-done = bf16[128,4096]{0,1:T(8,128)(2,1)} async-done(((bf16[128,64]{0,1:T(8,128)(2,1)}), bf16[128,4096]{0,1:T(8,128)(2,1)}) %all-gather.8.cloned.1.call-update) | async-done | bytes 1048592 | tf_op jit(solution)/shard_map/all_gather | solution.py:76
  382.7 2.0 bitcast_select_fusion
  384.7 0.5 stack.15
  385.2 56.0 %all_to_all.11 = bf16[64,128,128]{2,1,0:T(8,128)(2,1)S(1)} all-to-all(bf16[64,128,128]{2,1,0:T(8,128)(2,1)S(1)} %stack.15), channel_id=1, replica_groups=mesh['section'=8,'dp'=64] {'dp'}, dimensions={0} | all-to-all | bytes 4194304 | tf_op jit(solution)/shard_map/all_to_all | solution.py:85
  441.2 0.3 copy_bitcast_fusion
  441.6 3.3 collective-permute-start.1
  444.9 44.7 %collective-permute-done.1 = bf16[128,8192]{1,0:T(8,128)(2,1)S(1)} collective-permute-done((bf16[128,8192]{1,0:T(8,128)(2,1)S(1)}, bf16[128,8192]{1,0:T(8,128)(2,1)S(1)}, u32[]{:S(2)}, u32[]{:S(2)}) %collective-permute-start.1) | collective-permute-done | bytes 2097184 | tf_op jit(solution)/shard_map/ppermute | solution.py:12
  489.6 0.5 fusion.4
  490.1 1.1 fusion.21
  491.2 0.2 fusion.43
  491.5 1.1 copy-done.3
  492.6 3.6 fusion.62
  496.2 0.6 fusion.47
  496.8 0.0 all-gather.10.cloned.1.call-update
  496.9 82.7 %all-gather.10.cloned.1.call-done = bf16[128,4096]{0,1:T(8,128)(2,1)} async-done(((bf16[128,64]{0,1:T(8,128)(2,1)}), bf16[128,4096]{0,1:T(8,128)(2,1)}) %all-gather.10.cloned.1.call-update) | async-done | bytes 1048592 | tf_op jit(solution)/shard_map/all_gather | solution.py:76
  579.6 2.0 fusion.45
  581.6 0.7 maximum_bitcast_fusion
  (24 shorter events, 0.1 us)
Async XLA Ops:
  6.5 90.7 %copy-start = (bf16[1,3,64,8192]{3,2,1,0:T(8,128)(2,1)S(1)}, bf16[1,3,64,8192]{3,2,1,0:T(8,128)(2,1)}, u32[]{:S(2)}) copy-start(bf16[1,3,64,8192]{3,2,1,0:T(8,128)(2,1)} %param.11) | copy-start | bytes 9437188
  6.5 88.6 %all-gather.12.cloned.1.call-start = ((), (), s32[]{:S(2)}) async-start(), calls=%async_computation.5 | async-start | bytes 2129920 | tf_op jit(solution)/shard_map/all_gather | solution.py:65
  8.1 177.7 %all-gather.6.cloned.1.call-start = ((), (), s32[]{:S(2)}) async-start(), calls=%async_computation.2 | async-start | bytes 1064960 | tf_op jit(solution)/shard_map/all_gather | solution.py:76
  17.6 79.6 %copy-start.7 = (f32[1,8192]{1,0:T(1,128)S(1)}, f32[1,8192]{1,0:T(1,128)}, u32[]{:S(2)}) copy-start(f32[1,8192]{1,0:T(1,128)} %param.10) | copy-start | bytes 98308
  97.2 3.0 copy-start.1
  100.0 85.8 %copy-start.6 = (bf16[3,128,128]{2,1,0:T(8,128)(2,1)S(1)}, bf16[3,128,128]{2,1,0:T(8,128)(2,1)}, u32[]{:S(2)}) copy-start(bf16[3,128,128]{2,1,0:T(8,128)(2,1)} %param.8) | copy-start | bytes 294916
  104.5 278.2 %all-gather.8.cloned.1.call-start = ((), (), s32[]{:S(2)}) async-start(), calls=%async_computation.3 | async-start | bytes 1064960 | tf_op jit(solution)/shard_map/all_gather | solution.py:76
  244.7 48.1 %collective-permute-start = (bf16[128,8192]{1,0:T(8,128)(2,1)S(1)}, bf16[128,8192]{1,0:T(8,128)(2,1)S(1)}, u32[]{:S(2)}, u32[]{:S(2)}) collective-permute-start(bf16[128,8192]{1,0:T(8,128)(2,1)S(1)} %copy_bitcast_fusion.1), channel_id=1, source_target_pairs={{0,64},{64,128},{128,192},{192,256},{256,320},{320,384},{384,448},... | collective-permute-start | bytes 6291464 | tf_op jit(solution)/shard_map/ppermute | solution.py:12
  292.8 1.6 copy-start.4
  293.2 2.4 copy-start.2
  300.0 279.6 %all-gather.10.cloned.1.call-start = ((), (), s32[]{:S(2)}) async-start(), calls=%async_computation.4 | async-start | bytes 1064960 | tf_op jit(solution)/shard_map/all_gather | solution.py:76
  441.6 48.1 %collective-permute-start.1 = (bf16[128,8192]{1,0:T(8,128)(2,1)S(1)}, bf16[128,8192]{1,0:T(8,128)(2,1)S(1)}, u32[]{:S(2)}, u32[]{:S(2)}) collective-permute-start(bf16[128,8192]{1,0:T(8,128)(2,1)S(1)} %copy_bitcast_fusion), channel_id=1, source_target_pairs={{0,64},{64,128},{128,192},{192,256},{256,320},{320,384},{384,448},... | collective-permute-start | bytes 6291464 | tf_op jit(solution)/shard_map/ppermute | solution.py:12
  489.6 1.6 copy-start.5
  490.1 2.4 copy-start.3
Sparse Core Ops, SparseCore 0:
  10.6 84.5 all-gather.11
  104.6 81.1 all-gather.5
  300.1 82.5 all-gather.7
  497.0 82.5 all-gather.9
